TPU v7x, 512 devices: a whole 4x8x8 slice. The times are simulated.
512 devices in a mesh: round: 128 (over z, y, core), mp: 4 (over x).
Axes of the slice: x: 4, y: 8, z: 8, core: 2. Of those that a mesh axis runs over, the one named last changes fastest.
Arguments:
- tokens: bfloat16 [128, 512, 512], P('round'), may hold values from -8 to 8
- cell_order: int32 [512], replicated, may hold values from 0 to 511, each once
- seam_rows: int32 [128, 128, 2], P('round'), may hold values from -1 to 511, as said below
- obs_mask: int32 [16, 512], replicated, may hold values from 0 to 1, as said below
- norm_gain: float32 [512], replicated, may hold values from 0.1 to 1.9
- w_query: bfloat16 [512, 512], P(None, 'mp'), may hold values from -1 to 1
- w_key: bfloat16 [512, 512], P(None, 'mp'), may hold values from -1 to 1
- w_value: bfloat16 [512, 512], P(None, 'mp'), may hold values from -0.25 to 0.25
- w_out: bfloat16 [512, 512], P('mp'), may hold values from -0.25 to 0.25
- w_gate: bfloat16 [512, 2048], P(None, 'mp'), may hold values from -0.25 to 0.25
- w_up: bfloat16 [512, 2048], P(None, 'mp'), may hold values from -0.25 to 0.25
- w_down: bfloat16 [2048, 512], P('mp'), may hold values from -0.125 to 0.125
- w_read: float32 [512], replicated, may hold values from -0.25 to 0.25
Outputs:
- tiles_out: bfloat16 [128, 512, 512], P('mp', 'round')
- obs_logits: float32 [16], replicated
Inputs may be any that keep to these rules, and one draw needn't show every extreme that they name: `seam_rows`: each entry is a row of the sending tile or -1 for an empty slot; the live entries of one tile are all different; a tile's slots to itself are full, and some owner's slots are full from every tile. `obs_mask`: every observable's support holds at least one cell.
All inputs are finite; a program needn't handle non-finite values.
Results may differ from a plain program's by a relative error of at most 0.0052.
The roundings to bfloat16 on the way count: a program that leaves them out, or rounds other values in their place, can miss the bound.
Values may be sent and summed in bfloat16 or wider, within the bound.
A program may use at most 64 MiB of HBM per device.

v0:
```python
import math
import jax
import jax.numpy as jnp
from jax import lax
from jax.sharding import PartitionSpec as P

HDIM = 64
norm_eps = 1e-06


def normalize(rows_in, norm_gain):
    values = rows_in.astype(jnp.float32)
    spread = jnp.mean(values * values, axis=-1, keepdims=True)
    return (values * lax.rsqrt(spread + norm_eps) * norm_gain).astype(jnp.bfloat16)


def attend(queries, keys_all, values_all, live_keys):
    scale_factor = 1.0 / math.sqrt(queries.shape[-1])
    scores = (
        jnp.einsum("qhe,khe->hqk", queries, keys_all, preferred_element_type=jnp.float32)
        * scale_factor
    )
    if live_keys is not None:
        scores = jnp.where(live_keys[None, None, :], scores, -1e30)
    row_max = jnp.max(scores, axis=-1, keepdims=True)
    weights = jnp.exp(scores - row_max)
    probabilities = (weights / jnp.sum(weights, axis=-1, keepdims=True)).astype(jnp.bfloat16)
    mixture = jnp.einsum(
        "hqk,khe->qhe", probabilities, values_all, preferred_element_type=jnp.float32
    )
    return mixture.reshape(mixture.shape[0], -1)


def shards(
    tokens,
    cell_order,
    seam_rows,
    obs_mask,
    norm_gain,
    w_query,
    w_key,
    w_value,
    w_out,
    w_gate,
    w_up,
    w_down,
    w_read,
):
    round_count = lax.axis_size("round")
    model_count = lax.axis_size("mp")
    model_index = lax.axis_index("mp")
    round_index = lax.axis_index("round")
    width = tokens.shape[2]
    cell_dev = tokens.shape[1] // round_count
    permuted = tokens[:, cell_order, :]
    tile_tokens = lax.all_to_all(permuted, "round", split_axis=1, concat_axis=0, tiled=True)
    tile_rows = tile_tokens.shape[0] * cell_dev
    flat_tokens = tile_tokens.reshape(tile_rows, width)
    normed = normalize(flat_tokens, norm_gain)
    queries = jnp.dot(normed, w_query, preferred_element_type=jnp.float32).astype(jnp.bfloat16)
    keys_all = jnp.dot(normed, w_key, preferred_element_type=jnp.float32).astype(jnp.bfloat16)
    values_all = jnp.dot(normed, w_value, preferred_element_type=jnp.float32).astype(jnp.bfloat16)
    head_width = queries.shape[1]
    heads_dev = head_width // HDIM
    block_rows = min(512, tile_rows)
    query_blocks = queries.reshape(tile_rows // block_rows, block_rows, heads_dev, HDIM)
    key_heads = keys_all.reshape(tile_rows, heads_dev, HDIM)
    value_heads = values_all.reshape(tile_rows, heads_dev, HDIM)
    local_attn = lax.map(
        lambda query_block: attend(query_block, key_heads, value_heads, None), query_blocks
    )
    local_attn = local_attn.reshape(tile_rows, head_width)
    live_slot = seam_rows[0] >= 0
    safe_rows = jnp.where(live_slot, seam_rows[0], 0)
    packet = (
        lax.all_to_all(queries[safe_rows], "round", split_axis=0, concat_axis=0, tiled=True),
        lax.all_to_all(keys_all[safe_rows], "round", split_axis=0, concat_axis=0, tiled=True),
        lax.all_to_all(values_all[safe_rows], "round", split_axis=0, concat_axis=0, tiled=True),
        lax.all_to_all(
            live_slot.astype(jnp.bfloat16), "round", split_axis=0, concat_axis=0, tiled=True
        ),
    )
    seam_queries = packet[0].reshape(-1, heads_dev, HDIM)
    seam_keys = packet[1].reshape(-1, heads_dev, HDIM)
    seam_values = packet[2].reshape(-1, heads_dev, HDIM)
    seam_live = packet[3].reshape(-1) > 0.5
    seam_attn = attend(seam_queries, seam_keys, seam_values, seam_live).astype(jnp.bfloat16)
    returned = lax.all_to_all(
        seam_attn.reshape(round_count, -1, head_width),
        "round",
        split_axis=0,
        concat_axis=0,
        tiled=True,
    )
    target = jnp.where(live_slot, seam_rows[0], tile_rows).reshape(-1)
    combined = (
        local_attn.at[target]
        .add(returned.reshape(-1, head_width).astype(jnp.float32), mode="drop")
        .astype(jnp.bfloat16)
    )
    share_rows = tile_rows // model_count
    own_first = model_index * share_rows
    gate_part = jnp.dot(normed, w_gate, preferred_element_type=jnp.float32)
    up_part = jnp.dot(normed, w_up, preferred_element_type=jnp.float32)
    hidden = (jax.nn.silu(gate_part) * up_part).astype(jnp.bfloat16)
    attn_part = jnp.dot(combined, w_out, preferred_element_type=jnp.float32)
    summed = lax.psum_scatter(
        attn_part + jnp.dot(hidden, w_down, preferred_element_type=jnp.float32),
        "mp",
        scatter_dimension=0,
        tiled=True,
    )
    own_rows = lax.dynamic_slice_in_dim(flat_tokens, own_first, share_rows, 0)
    result_rows = (own_rows.astype(jnp.float32) + summed).astype(jnp.bfloat16)
    tiles_out = result_rows.reshape(share_rows // cell_dev, cell_dev, width)
    my_cells = lax.dynamic_slice_in_dim(cell_order, round_index * cell_dev, cell_dev)
    support = obs_mask[:, my_cells].astype(jnp.float32)
    partial_sum = jnp.einsum(
        "oc,rcd->od", support, tiles_out.astype(jnp.float32), precision=lax.Precision.HIGHEST
    )
    support_count = round_count * jnp.sum(obs_mask.astype(jnp.float32), axis=1)
    divisor = jnp.sqrt(support_count)
    pooled = lax.psum(partial_sum, ("round", "mp"))
    obs_logits = jnp.dot(pooled, w_read, precision=lax.Precision.HIGHEST) / divisor
    return (tiles_out, obs_logits)


def solution(mesh):
    return jax.shard_map(
        shards,
        mesh=mesh,
        in_specs=(
            P("round", None, None),
            P(),
            P("round", None, None),
            P(),
            P(),
            P(None, "mp"),
            P(None, "mp"),
            P(None, "mp"),
            P("mp", None),
            P(None, "mp"),
            P(None, "mp"),
            P("mp", None),
            P(),
        ),
        out_specs=(P("mp", "round", None), P()),
        check_vma=False,
    )
```

profile of v0, /device:TPU:1, one launch (start us, length us, event | category | flops | bytes accessed | tf_op | source)
XLA Modules:
  0.0 291.0 jit_solution(16656046799085090074)
XLA Ops:
  7.2 0.7 fusion.42
  7.9 0.8 copy.61
  8.7 18.4 %all-to-all-start.2 = ((bf16[128,1,2]{2,1,0:T(2,128)(2,1)}), bf16[128,1,2]{2,1,0:T(2,128)(2,1)S(1)}, u32[]{:S(2)}, u32[]{:S(2)}) async-start(bf16[128,1,2]{2,1,0:T(2,128)(2,1)} %copy.61), calls=%async_computation.2 | async-start | bytes 131072 | tf_op jit(solution)/shard_map/all_to_all | solution.py:79
  27.1 0.7 compare_select_fusion.2
  27.8 2.0 gather_fusion
  29.8 0.8 copy.95
  30.6 0.5 broadcast.153
  31.1 3.8 %reduce.2 = bf16[512,512]{1,0:T(8,128)(2,1)S(1)} reduce(bf16[512,1,512]{2,1,0:T(2,128)(2,1)S(1)} %bitcast.69, bf16[]{:T(256)} %broadcast.153), dimensions={1}, to_apply=%bitcast.66.reduce_sub_computation | reduce | bytes 1048578
  35.0 1.1 reshape.218
  36.1 2.4 all-to-all-done.2
  38.5 11.3 %all-to-all-start = ((bf16[128,2,1024]{2,1,0:T(2,128)(2,1)}), bf16[128,2,1024]{2,1,0:T(2,128)(2,1)S(1)}, u32[]{:S(2)}, u32[]{:S(2)}) async-start(bf16[128,2,1024]{2,1,0:T(2,128)(2,1)} %reshape.218), calls=%async_computation | async-start | bytes 1048576 | tf_op jit(solution)/shard_map/all_to_all | solution.py:56
  50.1 0.1 reshape.170
  50.2 0.1 squeeze.13
  50.4 0.2 compare_reduce_fusion
  50.6 0.1 gt.15
  50.8 19.6 %all-to-all-done = bf16[128,2,1024]{2,1,0:T(2,128)(2,1)S(1)} async-done(((bf16[128,2,1024]{2,1,0:T(2,128)(2,1)}), bf16[128,2,1024]{2,1,0:T(2,128)(2,1)S(1)}, u32[]{:S(2)}, u32[]{:S(2)}) %all-to-all-start) | async-done | bytes 524320 | tf_op jit(solution)/shard_map/all_to_all | solution.py:56
  70.4 0.4 reshape.219
  70.9 1.1 bitcast_convert_fusion
  72.0 0.1 fusion.9
  72.1 0.5 copy-done.7
  72.6 0.2 fusion.11
  72.8 0.2 copy-done.3
  73.0 0.3 convolution_convert_fusion.1
  73.3 0.2 copy-done.4
  73.5 0.3 convolution_convert_fusion.2
  74.0 0.1 copy.62
  74.1 1.5 gather_fusion.1
  75.6 1.5 gather_fusion.2
  77.0 6.3 %all-to-all-start.3 = ((bf16[128,2,128]{2,1,0:T(2,128)(2,1)}), bf16[128,2,128]{2,1,0:T(2,128)(2,1)}, u32[]{:S(2)}, u32[]{:S(2)}) async-start(bf16[128,2,128]{2,1,0:T(2,128)(2,1)} %bitcast.12), calls=%async_computation.3 | async-start | bytes 131072 | tf_op jit(solution)/shard_map/all_to_all | solution.py:76
  83.3 1.5 fusion.55
  84.8 1.0 convolution_convert_fusion
  85.8 1.0 copy.63
  86.8 1.5 gather_fusion.3
  88.3 5.8 %all-to-all-done.3 = bf16[128,2,128]{2,1,0:T(2,128)(2,1)} async-done(((bf16[128,2,128]{2,1,0:T(2,128)(2,1)}), bf16[128,2,128]{2,1,0:T(2,128)(2,1)}, u32[]{:S(2)}, u32[]{:S(2)}) %all-to-all-start.3) | async-done | bytes 65568 | tf_op jit(solution)/shard_map/all_to_all | solution.py:76
  94.1 8.0 %all-to-all-start.4 = ((bf16[128,2,128]{2,1,0:T(2,128)(2,1)}), bf16[128,2,128]{2,1,0:T(2,128)(2,1)}, u32[]{:S(2)}, u32[]{:S(2)}) async-start(bf16[128,2,128]{2,1,0:T(2,128)(2,1)} %bitcast.78), calls=%async_computation.4 | async-start | bytes 131072 | tf_op jit(solution)/shard_map/all_to_all | solution.py:77
  102.1 1.7 fusion.49
  103.9 0.9 reshape.151
  104.8 8.5 %all-to-all-done.4 = bf16[128,2,128]{2,1,0:T(2,128)(2,1)} async-done(((bf16[128,2,128]{2,1,0:T(2,128)(2,1)}), bf16[128,2,128]{2,1,0:T(2,128)(2,1)}, u32[]{:S(2)}, u32[]{:S(2)}) %all-to-all-start.4) | async-done | bytes 65568 | tf_op jit(solution)/shard_map/all_to_all | solution.py:77
  113.3 6.9 %all-to-all-start.1 = ((bf16[128,2,128]{2,1,0:T(2,128)(2,1)}), bf16[128,2,128]{2,1,0:T(2,128)(2,1)}, u32[]{:S(2)}, u32[]{:S(2)}) async-start(bf16[128,2,128]{2,1,0:T(2,128)(2,1)} %bitcast.76), calls=%async_computation.1 | async-start | bytes 131072 | tf_op jit(solution)/shard_map/all_to_all | solution.py:78
  120.2 1.6 reshape.152
  121.8 1.9 fusion.6
  123.7 1.2 fusion.50
  124.9 6.7 %all-to-all-done.1 = bf16[128,2,128]{2,1,0:T(2,128)(2,1)} async-done(((bf16[128,2,128]{2,1,0:T(2,128)(2,1)}), bf16[128,2,128]{2,1,0:T(2,128)(2,1)}, u32[]{:S(2)}, u32[]{:S(2)}) %all-to-all-start.1) | async-done | bytes 65568 | tf_op jit(solution)/shard_map/all_to_all | solution.py:78
  131.6 0.9 reshape.150
  132.6 2.1 fusion.7
  134.7 1.0 copy.68
  135.6 0.7 convert_element_type.92
  136.4 7.4 %all-to-all-start.5 = ((bf16[128,2,128]{2,1,0:T(2,128)(2,1)}), bf16[128,2,128]{2,1,0:T(2,128)(2,1)S(1)}, u32[]{:S(2)}, u32[]{:S(2)}) async-start(bf16[128,2,128]{2,1,0:T(2,128)(2,1)} %convert_element_type.92), calls=%async_computation.5 | async-start | bytes 131072 | tf_op jit(solution)/shard_map/all_to_all | solution.py:88
  143.8 2.7 fusion.18
  146.5 1.1 copy.69
  147.6 7.6 %all-to-all-done.5 = bf16[128,2,128]{2,1,0:T(2,128)(2,1)S(1)} async-done(((bf16[128,2,128]{2,1,0:T(2,128)(2,1)}), bf16[128,2,128]{2,1,0:T(2,128)(2,1)S(1)}, u32[]{:S(2)}, u32[]{:S(2)}) %all-to-all-start.5) | async-done | bytes 65568 | tf_op jit(solution)/shard_map/all_to_all | solution.py:88
  155.2 2.0 scatter_custom_fusion
  157.2 2.2 fusion.28
  159.4 3.3 %convolution_add_fusion = f32[512,512]{1,0:T(8,128)} fusion(f32[512,512]{1,0:T(8,128)} %fusion.28, bf16[512,512]{1,0:T(8,128)(2,1)} %param.24, bf16[512,512]{1,0:T(8,128)(2,1)S(1)} %fusion.11, bf16[512,512]{1,0:T(8,128)(2,1)} %param.23, f32[512,512]{1,0:T(8,128)S(1)} %fusion.55), kind=kOutput, calls=%fused_computation.12 | convolution fusion | flops 538705920 | bytes 4718592 | tf_op jit(solution)/shard_map/dot_general | solution.py:108
  162.8 0.7 copy-done.2
  163.5 0.1 copy.70
  163.6 0.8 compare_select_fusion.5
  164.4 0.6 gather_fusion.4
  165.1 0.3 constant_dynamic-slice_fusion
  165.3 18.2 %reduce-scatter.2.cloned.1.call-done = f32[128,512]{1,0:T(8,128)} async-done(((f32[512,512]{1,0:T(8,128)}), f32[128,512]{1,0:T(8,128)}) %reduce-scatter.2.cloned.1.call-update) | async-done | bytes 262160 | tf_op jit(solution)/shard_map/reduce_scatter | solution.py:107
  183.6 1.0 fusion.20
  184.7 0.2 fusion.38
  184.9 98.6 %psum.7 = f32[16,512]{1,0:T(8,128)S(1)} all-reduce(f32[16,512]{1,0:T(8,128)S(1)} %fusion.38), channel_id=1, replica_groups=mesh['round'=128,'mp'=4] {'round','mp'}, use_global_device_ids=true, to_apply=%region_8.9 | all-reduce | flops 8192 | bytes 65536 | tf_op jit(solution)/shard_map/psum | solution.py:123
  283.5 0.7 fusion.8
  (28 shorter events, 0.7 us)
Async XLA Ops:
  7.2 20.7 %copy-start = (bf16[1,512,512]{2,1,0:T(8,128)(2,1)S(1)}, bf16[1,512,512]{2,1,0:T(8,128)(2,1)}, u32[]{:S(2)}) copy-start(bf16[1,512,512]{2,1,0:T(8,128)(2,1)} %param.13) | copy-start | bytes 1572868
  8.7 29.8 %all-to-all-start.2 = ((bf16[128,1,2]{2,1,0:T(2,128)(2,1)}), bf16[128,1,2]{2,1,0:T(2,128)(2,1)S(1)}, u32[]{:S(2)}, u32[]{:S(2)}) async-start(bf16[128,1,2]{2,1,0:T(2,128)(2,1)} %copy.61), calls=%async_computation.2 | async-start | bytes 131072 | tf_op jit(solution)/shard_map/all_to_all | solution.py:79
  35.0 14.9 %copy-start.6 = (s32[1,128,2]{1,2,0:T(2,128)S(1)}, s32[1,128,2]{1,2,0:T(2,128)}, u32[]{:S(2)}) copy-start(s32[1,128,2]{1,2,0:T(2,128)} %param.15) | copy-start | bytes 3076
  38.5 31.9 %all-to-all-start = ((bf16[128,2,1024]{2,1,0:T(2,128)(2,1)}), bf16[128,2,1024]{2,1,0:T(2,128)(2,1)S(1)}, u32[]{:S(2)}, u32[]{:S(2)}) async-start(bf16[128,2,1024]{2,1,0:T(2,128)(2,1)} %reshape.218), calls=%async_computation | async-start | bytes 1048576 | tf_op jit(solution)/shard_map/all_to_all | solution.py:56
  71.9 0.7 copy-start.7
  72.1 0.9 copy-start.3
  72.6 0.9 copy-start.4
  77.0 17.0 %all-to-all-start.3 = ((bf16[128,2,128]{2,1,0:T(2,128)(2,1)}), bf16[128,2,128]{2,1,0:T(2,128)(2,1)}, u32[]{:S(2)}, u32[]{:S(2)}) async-start(bf16[128,2,128]{2,1,0:T(2,128)(2,1)} %bitcast.12), calls=%async_computation.3 | async-start | bytes 131072 | tf_op jit(solution)/shard_map/all_to_all | solution.py:76
  83.3 1.5 copy-start.5
  94.1 19.2 %all-to-all-start.4 = ((bf16[128,2,128]{2,1,0:T(2,128)(2,1)}), bf16[128,2,128]{2,1,0:T(2,128)(2,1)}, u32[]{:S(2)}, u32[]{:S(2)}) async-start(bf16[128,2,128]{2,1,0:T(2,128)(2,1)} %bitcast.78), calls=%async_computation.4 | async-start | bytes 131072 | tf_op jit(solution)/shard_map/all_to_all | solution.py:77
  113.3 18.3 %all-to-all-start.1 = ((bf16[128,2,128]{2,1,0:T(2,128)(2,1)}), bf16[128,2,128]{2,1,0:T(2,128)(2,1)}, u32[]{:S(2)}, u32[]{:S(2)}) async-start(bf16[128,2,128]{2,1,0:T(2,128)(2,1)} %bitcast.76), calls=%async_computation.1 | async-start | bytes 131072 | tf_op jit(solution)/shard_map/all_to_all | solution.py:78
  136.4 18.8 %all-to-all-start.5 = ((bf16[128,2,128]{2,1,0:T(2,128)(2,1)}), bf16[128,2,128]{2,1,0:T(2,128)(2,1)S(1)}, u32[]{:S(2)}, u32[]{:S(2)}) async-start(bf16[128,2,128]{2,1,0:T(2,128)(2,1)} %convert_element_type.92), calls=%async_computation.5 | async-start | bytes 131072 | tf_op jit(solution)/shard_map/all_to_all | solution.py:88
  143.8 39.8 %reduce-scatter.2.cloned.1.call-start = ((), (), s32[]{:S(2)}) async-start(), calls=%async_computation.7 | async-start | bytes 1310720 | tf_op jit(solution)/shard_map/reduce_scatter | solution.py:107
  162.7 0.8 copy-start.2
  163.5 120.0 %copy-start.8 = (f32[512]{0:T(512)S(1)}, f32[512]{0:T(512)}, u32[]{:S(2)}) copy-start(f32[512]{0:T(512)} %param.25) | copy-start | bytes 6148
  184.6 99.6 %copy-start.1 = (bf16[32,4,512]{2,1,0:T(4,128)(2,1)}, bf16[32,4,512]{2,1,0:T(4,128)(2,1)S(1)}, u32[]{:S(2)}) copy-start(bf16[32,4,512]{2,1,0:T(4,128)(2,1)S(1)} %reshape.153) | copy-start | bytes 393220
Sparse Core Ops, SparseCore 0:
  162.9 20.6 reduce-scatter.1
where the time goes:
time: 292 us; the launch traced here: 291 us
  blocking collectives  98.6 us (34%)
  waiting for transfers between devices  68.8 us (24%)
  starting transfers between devices  58.4 us (20%)
  local copies, waits for them, and re-layouts  20.8 us (7%)
  matrix products  19.2 us (7%)
  between operations  14.4 us (5%)
  other arithmetic  10.9 us (4%)
    psum x1, blocking collectives, shards(): pooled = lax.psum(partial_sum, ('round', 'mp'))  98.6 us
    all_to_all x1, waiting for transfers between devices, shards(): lax.all_to_all(permuted, 'round', split_axis=1, concat_axis=0, tiled=True)  19.6 us
    all_to_all x1, starting transfers between devices, shards(): lax.all_to_all(live_slot.astype(jnp.bfloat16), 'round', split_axis=0, con...  18.4 us
    reduce_scatter x1, waiting for transfers between devices, shards(): lax.psum_scatter(attn_part + jnp.dot(hidden, w_down, preferred_element_ty...  18.2 us
    all_to_all x1, starting transfers between devices, shards(): lax.all_to_all(permuted, 'round', split_axis=1, concat_axis=0, tiled=True)  11.3 us
    all_to_all x1, waiting for transfers between devices, shards(): lax.all_to_all(keys_all[safe_rows], 'round', split_axis=0, concat_axis=0,...  8.46 us
    all_to_all x1, starting transfers between devices, shards(): lax.all_to_all(keys_all[safe_rows], 'round', split_axis=0, concat_axis=0,...  8.03 us
    all_to_all x1, waiting for transfers between devices, shards(): lax.all_to_all(seam_attn.reshape(round_count, -1, head_width), 'round', s...  7.59 us
  transfers between devices with their start and end apart: 7, of which 7 were waited for; matrix products, arithmetic and copies ran while one was open for 10% of the time, Pallas kernels for 0%

commit v1 on v0

--- a/solution.py
+++ b/solution.py
@@ -120,7 +120,8 @@
     )
     support_count = round_count * jnp.sum(obs_mask.astype(jnp.float32), axis=1)
     divisor = jnp.sqrt(support_count)
-    pooled = lax.psum(partial_sum, ("round", "mp"))
+    parts = lax.all_gather(partial_sum, ("round", "mp"), axis=0, tiled=False)
+    pooled = parts.sum(axis=0)
     obs_logits = jnp.dot(pooled, w_read, precision=lax.Precision.HIGHEST) / divisor
     return (tiles_out, obs_logits)
 

time: 292 us -> 342 us (1.17)
  waiting for transfers between devices: 68.8 us -> 208 us
  blocking collectives: 98.6 us -> 0 us
  other arithmetic: 10.9 us -> 18 us
    all_gather x0 -> x1, waiting for transfers between devices: none -> 140 us  [shards(): parts = lax.all_gather(partial_sum, ('round', 'mp'), axis=0, tiled=False)]
    psum x1 -> x0, blocking collectives: 98.6 us -> none  [shards(): pooled = lax.psum(partial_sum, ('round', 'mp'))]
    reduce_sum x0 -> x1, other arithmetic: none -> 6.78 us  [shards(): pooled = parts.sum(axis=0)]
  transfers between devices with their start and end apart: 7 -> 8, of which waited for: 7 -> 8; matrix products, arithmetic and copies ran while one was open for 10% -> 9% of each run, Pallas kernels for 0% -> 0%
where the time goes in v1:
time: 342 us; the launch traced here: 341 us
  waiting for transfers between devices  208 us (61%)
  starting transfers between devices  61.6 us (18%)
  matrix products  19.8 us (6%)
  local copies, waits for them, and re-layouts  19.2 us (6%)
  other arithmetic  18 us (5%)
  between operations  14.4 us (4%)
    all_gather x1, waiting for transfers between devices, shards(): parts = lax.all_gather(partial_sum, ('round', 'mp'), axis=0, tiled=False)  140 us
    all_to_all x1, waiting for transfers between devices, shards(): lax.all_to_all(permuted, 'round', split_axis=1, concat_axis=0, tiled=True)  19.6 us
    reduce_scatter x1, waiting for transfers between devices, shards(): lax.psum_scatter(attn_part + jnp.dot(hidden, w_down, preferred_element_ty...  19.3 us
    all_to_all x1, starting transfers between devices, shards(): lax.all_to_all(live_slot.astype(jnp.bfloat16), 'round', split_axis=0, con...  18.4 us
    all_to_all x1, starting transfers between devices, shards(): lax.all_to_all(permuted, 'round', split_axis=1, concat_axis=0, tiled=True)  11.3 us
    all_to_all x1, starting transfers between devices, shards(): lax.all_to_all(keys_all[safe_rows], 'round', split_axis=0, concat_axis=0,...  10.8 us
    all_to_all x1, waiting for transfers between devices, shards(): lax.all_to_all(keys_all[safe_rows], 'round', split_axis=0, concat_axis=0,...  9.36 us
    all_to_all x1, starting transfers between devices, shards(): lax.all_to_all(seam_attn.reshape(round_count, -1, head_width), 'round', s...  7.86 us
  transfers between devices with their start and end apart: 8, of which 8 were waited for; matrix products, arithmetic and copies ran while one was open for 9% of the time, Pallas kernels for 0%

profile of v1, /device:TPU:1, one launch (start us, length us, event | category | flops | bytes accessed | tf_op | source)
XLA Modules:
  0.0 340.9 jit_solution(12342153771098729261)
XLA Ops:
  7.2 0.7 fusion.42
  7.9 0.8 copy.61
  8.7 18.4 %all-to-all-start.2 = ((bf16[128,1,2]{2,1,0:T(2,128)(2,1)}), bf16[128,1,2]{2,1,0:T(2,128)(2,1)S(1)}, u32[]{:S(2)}, u32[]{:S(2)}) async-start(bf16[128,1,2]{2,1,0:T(2,128)(2,1)} %copy.61), calls=%async_computation.2 | async-start | bytes 131072 | tf_op jit(solution)/shard_map/all_to_all | solution.py:79
  27.1 0.7 compare_select_fusion.2
  27.8 2.0 gather_fusion
  29.8 0.8 copy.95
  30.6 0.5 broadcast.153
  31.1 3.8 %reduce.2 = bf16[512,512]{1,0:T(8,128)(2,1)S(1)} reduce(bf16[512,1,512]{2,1,0:T(2,128)(2,1)S(1)} %bitcast.71, bf16[]{:T(256)} %broadcast.153), dimensions={1}, to_apply=%bitcast.67.reduce_sub_computation | reduce | bytes 1048578
  35.0 1.1 reshape.219
  36.1 2.4 all-to-all-done.2
  38.5 11.3 %all-to-all-start = ((bf16[128,2,1024]{2,1,0:T(2,128)(2,1)}), bf16[128,2,1024]{2,1,0:T(2,128)(2,1)S(1)}, u32[]{:S(2)}, u32[]{:S(2)}) async-start(bf16[128,2,1024]{2,1,0:T(2,128)(2,1)} %reshape.219), calls=%async_computation | async-start | bytes 1048576 | tf_op jit(solution)/shard_map/all_to_all | solution.py:56
  50.0 0.1 copy.59
  50.1 0.1 reshape.170
  50.2 0.1 squeeze.13
  50.4 0.2 compare_reduce_fusion
  50.6 0.1 gt.15
  50.8 19.6 %all-to-all-done = bf16[128,2,1024]{2,1,0:T(2,128)(2,1)S(1)} async-done(((bf16[128,2,1024]{2,1,0:T(2,128)(2,1)}), bf16[128,2,1024]{2,1,0:T(2,128)(2,1)S(1)}, u32[]{:S(2)}, u32[]{:S(2)}) %all-to-all-start) | async-done | bytes 524320 | tf_op jit(solution)/shard_map/all_to_all | solution.py:56
  70.4 0.4 reshape.220
  70.9 1.1 bitcast_convert_fusion
  72.0 0.1 fusion.9
  72.1 0.2 fusion.11
  72.3 0.3 convolution_convert_fusion.1
  72.6 0.1 copy.62
  72.7 1.5 gather_fusion.2
  74.2 6.2 %all-to-all-start.3 = ((bf16[128,2,128]{2,1,0:T(2,128)(2,1)}), bf16[128,2,128]{2,1,0:T(2,128)(2,1)}, u32[]{:S(2)}, u32[]{:S(2)}) async-start(bf16[128,2,128]{2,1,0:T(2,128)(2,1)} %bitcast.12), calls=%async_computation.3 | async-start | bytes 131072 | tf_op jit(solution)/shard_map/all_to_all | solution.py:76
  80.5 0.3 convolution_convert_fusion
  80.8 0.1 copy.63
  80.9 1.5 gather_fusion.3
  82.4 1.5 fusion.55
  83.9 1.9 convolution_convert_fusion.2
  85.7 1.0 copy.60
  86.8 1.5 gather_fusion.1
  88.2 3.0 all-to-all-done.3
  91.3 10.8 %all-to-all-start.4 = ((bf16[128,2,128]{2,1,0:T(2,128)(2,1)}), bf16[128,2,128]{2,1,0:T(2,128)(2,1)}, u32[]{:S(2)}, u32[]{:S(2)}) async-start(bf16[128,2,128]{2,1,0:T(2,128)(2,1)} %bitcast.79), calls=%async_computation.4 | async-start | bytes 131072 | tf_op jit(solution)/shard_map/all_to_all | solution.py:77
  102.1 0.8 fusion.49
  102.9 0.9 reshape.151
  103.9 9.4 %all-to-all-done.4 = bf16[128,2,128]{2,1,0:T(2,128)(2,1)} async-done(((bf16[128,2,128]{2,1,0:T(2,128)(2,1)}), bf16[128,2,128]{2,1,0:T(2,128)(2,1)}, u32[]{:S(2)}, u32[]{:S(2)}) %all-to-all-start.4) | async-done | bytes 65568 | tf_op jit(solution)/shard_map/all_to_all | solution.py:77
  113.2 6.9 %all-to-all-start.1 = ((bf16[128,2,128]{2,1,0:T(2,128)(2,1)}), bf16[128,2,128]{2,1,0:T(2,128)(2,1)}, u32[]{:S(2)}, u32[]{:S(2)}) async-start(bf16[128,2,128]{2,1,0:T(2,128)(2,1)} %bitcast.78), calls=%async_computation.1 | async-start | bytes 131072 | tf_op jit(solution)/shard_map/all_to_all | solution.py:78
  120.1 1.6 reshape.152
  121.7 1.9 fusion.6
  123.6 1.2 fusion.50
  124.9 6.7 %all-to-all-done.1 = bf16[128,2,128]{2,1,0:T(2,128)(2,1)} async-done(((bf16[128,2,128]{2,1,0:T(2,128)(2,1)}), bf16[128,2,128]{2,1,0:T(2,128)(2,1)}, u32[]{:S(2)}, u32[]{:S(2)}) %all-to-all-start.1) | async-done | bytes 65568 | tf_op jit(solution)/shard_map/all_to_all | solution.py:78
  131.6 0.9 reshape.150
  132.5 2.1 fusion.7
  134.6 1.0 copy.68
  135.6 0.7 convert_element_type.92
  136.3 7.9 %all-to-all-start.5 = ((bf16[128,2,128]{2,1,0:T(2,128)(2,1)}), bf16[128,2,128]{2,1,0:T(2,128)(2,1)}, u32[]{:S(2)}, u32[]{:S(2)}) async-start(bf16[128,2,128]{2,1,0:T(2,128)(2,1)} %convert_element_type.92), calls=%async_computation.5 | async-start | bytes 131072 | tf_op jit(solution)/shard_map/all_to_all | solution.py:88
  144.2 2.7 fusion.18
  146.9 1.1 copy.69
  148.0 7.3 %all-to-all-done.5 = bf16[128,2,128]{2,1,0:T(2,128)(2,1)} async-done(((bf16[128,2,128]{2,1,0:T(2,128)(2,1)}), bf16[128,2,128]{2,1,0:T(2,128)(2,1)}, u32[]{:S(2)}, u32[]{:S(2)}) %all-to-all-start.5) | async-done | bytes 65568 | tf_op jit(solution)/shard_map/all_to_all | solution.py:88
  155.3 2.3 scatter_custom_fusion
  157.7 2.2 fusion.28
  159.9 3.3 convolution_add_fusion
  163.3 0.1 copy.70
  163.4 0.8 compare_select_fusion.5
  164.2 0.6 gather_fusion.4
  164.7 0.3 constant_dynamic-slice_fusion
  165.0 19.3 %reduce-scatter.2.cloned.1.call-done = f32[128,512]{1,0:T(8,128)} async-done(((f32[512,512]{1,0:T(8,128)}), f32[128,512]{1,0:T(8,128)}) %reduce-scatter.2.cloned.1.call-update) | async-done | bytes 262160 | tf_op jit(solution)/shard_map/reduce_scatter | solution.py:107
  184.3 1.0 fusion.20
  185.4 0.8 fusion.38
  186.3 0.1 convert_reduce_fusion.1
  186.4 140.2 %all-gather.3.cloned.1.call-done = f32[8192,512]{1,0:T(8,128)} async-done(((f32[16,512]{1,0:T(8,128)}), f32[8192,512]{1,0:T(8,128)}) %all-gather.3.cloned.1.call-update) | async-done | bytes 16777232 | tf_op jit(solution)/shard_map/all_gather | solution.py:123
  326.6 6.8 %reduce_sum.59 = f32[16,512]{1,0:T(8,128)S(1)} reduce(f32[512,16,512]{2,1,0:T(8,128)} %bitcast.69, f32[]{:T(128)} %constant.20.clone.1), dimensions={0}, to_apply=%region_8.9 | reduce | flops 4186112 | bytes 16809988 | tf_op jit(solution)/shard_map/reduce_sum | solution.py:124
  333.4 0.7 fusion.8
  (29 shorter events, 0.4 us)
Async XLA Ops:
  7.2 20.7 %copy-start = (bf16[1,512,512]{2,1,0:T(8,128)(2,1)S(1)}, bf16[1,512,512]{2,1,0:T(8,128)(2,1)}, u32[]{:S(2)}) copy-start(bf16[1,512,512]{2,1,0:T(8,128)(2,1)} %param.13) | copy-start | bytes 1572868
  8.7 29.8 %all-to-all-start.2 = ((bf16[128,1,2]{2,1,0:T(2,128)(2,1)}), bf16[128,1,2]{2,1,0:T(2,128)(2,1)S(1)}, u32[]{:S(2)}, u32[]{:S(2)}) async-start(bf16[128,1,2]{2,1,0:T(2,128)(2,1)} %copy.61), calls=%async_computation.2 | async-start | bytes 131072 | tf_op jit(solution)/shard_map/all_to_all | solution.py:79
  30.6 19.2 %copy-start.5 = (s32[1,128,2]{1,2,0:T(2,128)S(1)}, s32[1,128,2]{1,2,0:T(2,128)}, u32[]{:S(2)}) copy-start(s32[1,128,2]{1,2,0:T(2,128)} %param.15) | copy-start | bytes 3076
  38.5 31.9 %all-to-all-start = ((bf16[128,2,1024]{2,1,0:T(2,128)(2,1)}), bf16[128,2,1024]{2,1,0:T(2,128)(2,1)S(1)}, u32[]{:S(2)}, u32[]{:S(2)}) async-start(bf16[128,2,1024]{2,1,0:T(2,128)(2,1)} %reshape.219), calls=%async_computation | async-start | bytes 1048576 | tf_op jit(solution)/shard_map/all_to_all | solution.py:56
  50.8 21.4 %copy-start.6 = (f32[512]{0:T(512)S(1)}, f32[512]{0:T(512)}, u32[]{:S(2)}) copy-start(f32[512]{0:T(512)} %param.17) | copy-start | bytes 6148
  70.9 1.4 copy-start.3
  72.0 8.5 %copy-start.4 = (bf16[512,128]{1,0:T(8,128)(2,1)S(1)}, bf16[512,128]{1,0:T(8,128)(2,1)}, u32[]{:S(2)}) copy-start(bf16[512,128]{1,0:T(8,128)(2,1)} %param.19) | copy-start | bytes 393220
  74.2 17.1 %all-to-all-start.3 = ((bf16[128,2,128]{2,1,0:T(2,128)(2,1)}), bf16[128,2,128]{2,1,0:T(2,128)(2,1)}, u32[]{:S(2)}, u32[]{:S(2)}) async-start(bf16[128,2,128]{2,1,0:T(2,128)(2,1)} %bitcast.12), calls=%async_computation.3 | async-start | bytes 131072 | tf_op jit(solution)/shard_map/all_to_all | solution.py:76
  91.3 22.0 %all-to-all-start.4 = ((bf16[128,2,128]{2,1,0:T(2,128)(2,1)}), bf16[128,2,128]{2,1,0:T(2,128)(2,1)}, u32[]{:S(2)}, u32[]{:S(2)}) async-start(bf16[128,2,128]{2,1,0:T(2,128)(2,1)} %bitcast.79), calls=%async_computation.4 | async-start | bytes 131072 | tf_op jit(solution)/shard_map/all_to_all | solution.py:77
  113.2 18.3 %all-to-all-start.1 = ((bf16[128,2,128]{2,1,0:T(2,128)(2,1)}), bf16[128,2,128]{2,1,0:T(2,128)(2,1)}, u32[]{:S(2)}, u32[]{:S(2)}) async-start(bf16[128,2,128]{2,1,0:T(2,128)(2,1)} %bitcast.78), calls=%async_computation.1 | async-start | bytes 131072 | tf_op jit(solution)/shard_map/all_to_all | solution.py:78
  136.3 19.0 %all-to-all-start.5 = ((bf16[128,2,128]{2,1,0:T(2,128)(2,1)}), bf16[128,2,128]{2,1,0:T(2,128)(2,1)}, u32[]{:S(2)}, u32[]{:S(2)}) async-start(bf16[128,2,128]{2,1,0:T(2,128)(2,1)} %convert_element_type.92), calls=%async_computation.5 | async-start | bytes 131072 | tf_op jit(solution)/shard_map/all_to_all | solution.py:88
  144.2 40.1 %reduce-scatter.2.cloned.1.call-start = ((), (), s32[]{:S(2)}) async-start(), calls=%async_computation.7 | async-start | bytes 1310720 | tf_op jit(solution)/shard_map/reduce_scatter | solution.py:107
  159.9 3.4 copy-start.2
  163.2 163.4 %all-gather.3.cloned.1.call-start = ((), (), s32[]{:S(2)}) async-start(), calls=%async_computation.8 | async-start | bytes 16809984 | tf_op jit(solution)/shard_map/all_gather | solution.py:123
  185.3 148.1 %copy-start.1 = (bf16[32,4,512]{2,1,0:T(4,128)(2,1)}, bf16[32,4,512]{2,1,0:T(4,128)(2,1)S(1)}, u32[]{:S(2)}) copy-start(bf16[32,4,512]{2,1,0:T(4,128)(2,1)S(1)} %reshape.153) | copy-start | bytes 393220
  326.6 6.8 %copy-start.7 = (f32[512]{0:T(512)S(1)}, f32[512]{0:T(512)}, u32[]{:S(2)}) copy-start(f32[512]{0:T(512)} %param.25) | copy-start | bytes 6148
Sparse Core Ops, SparseCore 0:
  163.3 20.9 reduce-scatter.1
  189.7 136.8 all-gather.2
